TPU v7x, 256 devices: a whole 4x4x8 slice. The times are simulated.
256 devices in a mesh: sec: 2 (over y_lo), grp: 16 (over z, y_hi), tp: 8 (over x, core).
Axes of the slice: x: 4, y: 4 (y_hi: 2, y_lo: 2; y = y_hi * 2 + y_lo), z: 8, core: 2. Of those that a mesh axis runs over, the one named last changes fastest.
Arguments:
- hidden_in: bfloat16 [1024, 7168], P(('sec', 'grp', 'tp')), may hold values from -6 to 6
- queries: bfloat16 [1024, 16, 8, 576], P(('sec', 'grp'), None, 'tp'), may hold values from -61 to 61
- latent_cache: bfloat16 [1024, 64, 576], P(('sec', 'grp')), may hold values from -6 to 6
- lengths: int32 [1024], P(('sec', 'grp')), may hold values from 2 to 64, as said below
- w_uv: bfloat16 [16, 8, 512, 128], P(None, 'tp'), may hold values from -0.75 to 0.75
- attn_weight: bfloat16 [16, 8, 128, 7168], P(None, 'tp', None, 'grp'), may hold values from -0.125 to 0.125
- norm_gain: float32 [7168], replicated, may hold values from 0.1 to 1.9
- router: bfloat16 [7168, 32], replicated, may hold values from -0.0625 to 0.0625
- routes: int32 [1024, 8], P(('sec', 'grp', 'tp')), may hold values from 0 to 31, all different within a row; in each aligned block of 4 rows (0 to 3, 4 to 7, ...) at most 2 rows name the same one
- live_counts: int32 [256], P(('sec', 'grp', 'tp')), may hold values from 3 to 4, as said below
- expert_in: bfloat16 [32, 7168, 2, 1024], P(('sec', 'grp'), None, None, 'tp'), may hold values from -0.0625 to 0.0625
- expert_out: bfloat16 [32, 1024, 7168], P(('sec', 'grp'), 'tp'), may hold values from -0.5 to 0.5
Outputs:
- layer_out: bfloat16 [1024, 7168], P(('sec', 'grp', 'tp'))
Inputs may be any that keep to these rules, and one draw needn't show every extreme that they name: `lengths`: some request has exactly 64 cached positions and some has 2. `live_counts`: some device has all 4 slots live and some has exactly 3. `routes`: the 8 experts of a token differ. Within the rows of one device (aligned blocks of 4 rows) no expert is named by more than 2 rows, a bound that some block reaches.
All inputs are finite; a program needn't handle non-finite values.
Results may differ from a plain program's by a relative error of at most 0.018.
Values may be sent and summed in bfloat16 or wider, within the bound.
No kernel may reach another device: no remote copies, remote signals or barrier semaphores. Data moves between devices by JAX's collectives and lax.ppermute only.
A program may use at most 64 MiB of HBM per device.

v0:
```python
import jax
import jax.numpy as jnp
from jax import lax
from jax.sharding import Mesh
from jax.sharding import PartitionSpec as P

GRP = ("grp_0", "grp_1")
SEC_GRP = ("sec", "grp_0", "grp_1")
GRP_SEC = ("grp_0", "grp_1", "sec")
SEC_GRP_TP = ("sec", "grp_0", "grp_1", "tp")
score_scale = 192.0 ** (-0.5)
route_scale = 2.5


def gathered_by_axis(x, axes, dim):
    out = x
    for number in range(len(axes) - 1, -1, -1):
        out = lax.all_gather(out, axes[number], axis=dim, tiled=True)
    return out


def in_blocks(x, dim, peers):
    lengths = x.shape
    tiles = x.reshape(*lengths[:dim], peers, lengths[dim] // peers, *lengths[dim + 1 :])
    return jnp.moveaxis(tiles, dim, 0)


def sent_and_summed(x, axis, dim):
    tiles = in_blocks(x, dim, lax.axis_size(axis))
    arrived = lax.all_to_all(tiles, axis, split_axis=0, concat_axis=0, tiled=True)
    return arrived.astype(jnp.float32).sum(axis=0)


def in_order(tiles, dim):
    tiles = jnp.moveaxis(tiles, 0, dim)
    lengths = tiles.shape
    return tiles.reshape(*lengths[:dim], lengths[dim] * lengths[dim + 1], *lengths[dim + 2 :])


def exchange_both(x, axis, axes, splits, concats):
    sizes = [lax.axis_size(a) for a in axes]
    tiles = in_blocks(x, splits[0], sizes[0])
    tiles = jnp.moveaxis(in_blocks(tiles, splits[1] + 1, sizes[1]), 0, 1)
    inside = tiles.shape[2:]
    tiles = tiles.reshape(-1, *inside)
    tiles = lax.all_to_all(tiles, axis, split_axis=0, concat_axis=0, tiled=True)
    tiles = in_order(tiles.reshape(*sizes, *inside), concats[0] + 1)
    return in_order(tiles, concats[1])


def expert_slice(rows_in, expert_in, expert_out):
    width = rows_in.shape[1]
    slice_width = expert_in.shape[3]
    gate_up = jnp.dot(
        rows_in, expert_in[0].reshape(width, 2 * slice_width), preferred_element_type=jnp.float32
    )
    activated = (jax.nn.silu(gate_up[:, :slice_width]) * gate_up[:, slice_width:]).astype(
        jnp.bfloat16
    )
    return jnp.dot(activated, expert_out[0], preferred_element_type=jnp.float32).astype(
        jnp.bfloat16
    )


def shards(
    hidden_in,
    queries,
    latent_cache,
    lengths,
    w_uv,
    attn_weight,
    norm_gain,
    router,
    routes,
    live_counts,
    expert_in,
    expert_out,
):
    count_of_tokens, width = hidden_in.shape
    sections = lax.axis_size("sec")
    expert_groups = lax.axis_size(GRP)
    slices = lax.axis_size("tp")
    latent_width = w_uv.shape[2]
    query_block = queries[:, :, 0, :]
    scores = (
        jnp.einsum("bhr,bpr->bhp", query_block, latent_cache, preferred_element_type=jnp.float32)
        * score_scale
    )
    positions = jnp.arange(latent_cache.shape[1])
    visible = positions[None, None, :] < lengths[:, None, None]
    scores = jnp.where(visible, scores, -1e30)
    highest = jnp.max(scores, axis=2, keepdims=True)
    raised = jnp.exp(scores - highest)
    softmax_weights = (raised / jnp.sum(raised, axis=2, keepdims=True)).astype(jnp.bfloat16)
    latent_out = jnp.einsum(
        "bhp,bpc->bhc",
        softmax_weights,
        latent_cache[:, :, :latent_width],
        preferred_element_type=jnp.float32,
    ).astype(jnp.bfloat16)
    head_out = jnp.einsum(
        "bhc,hcv->bhv", latent_out, w_uv[:, 0], preferred_element_type=jnp.float32
    ).astype(jnp.bfloat16)
    head_rows = head_out.reshape(head_out.shape[0], -1)
    out_block = attn_weight[:, 0].reshape(-1, attn_weight.shape[3])
    partial_value = jnp.dot(
        gathered_by_axis(head_rows, GRP, 0), out_block, preferred_element_type=jnp.float32
    )
    partial_value = partial_value.reshape(
        expert_groups, slices, count_of_tokens, partial_value.shape[1]
    )
    summed = sent_and_summed(partial_value.astype(jnp.bfloat16), "tp", 1)
    column_part = summed[:, 0].astype(jnp.bfloat16)
    attention = lax.all_to_all(column_part, GRP, split_axis=0, concat_axis=2, tiled=True)[0]
    residual = hidden_in.astype(jnp.float32) + attention.astype(jnp.float32)
    normalized_input = (
        residual
        * lax.rsqrt(jnp.mean(residual * residual, axis=1, keepdims=True) + 1e-06)
        * norm_gain
    ).astype(jnp.bfloat16)
    experts = router.shape[1]
    per_token = routes.shape[1]
    capacity = max(2, 2 * count_of_tokens * per_token // experts)
    affinity = jax.nn.sigmoid(jnp.dot(normalized_input, router, preferred_element_type=jnp.float32))
    picked = routes[:, :, None] == jnp.arange(experts)[None, None, :]
    chosen = jnp.sum(jnp.where(picked, affinity[:, None, :], 0.0), axis=2)
    living = jnp.arange(count_of_tokens) < live_counts[0]
    gate_weights = (
        route_scale
        * chosen
        / jnp.sum(chosen, axis=1, keepdims=True)
        * living[:, None].astype(jnp.float32)
    )
    routed = jnp.any(picked, axis=1) & living[:, None]
    routed_count = routed.astype(jnp.int32)
    slot_index = jnp.cumsum(routed_count, axis=0) - routed_count
    placed_tokens = routed[:, :, None] & (
        slot_index[:, :, None] == jnp.arange(capacity)[None, None, :]
    )
    expert_gate = jnp.sum(jnp.where(picked, gate_weights[:, :, None], 0.0), axis=1)
    outgoing = jnp.einsum(
        "poy,pj->oyj",
        placed_tokens.astype(jnp.bfloat16),
        normalized_input,
        preferred_element_type=jnp.float32,
    ).astype(jnp.bfloat16)
    combine_rows = (placed_tokens.astype(jnp.float32) * expert_gate[:, :, None]).reshape(
        count_of_tokens, experts * capacity
    )
    once_rows = outgoing.reshape(sections, expert_groups, capacity, width)
    arrived = exchange_both(once_rows, SEC_GRP, ("sec", GRP), (0, 1), (0, 1))
    local_rows = arrived.reshape(-1, width)
    every_out = expert_slice(
        lax.all_gather(local_rows, "tp", axis=0, tiled=True), expert_in, expert_out
    )
    own_sums = lax.psum_scatter(
        every_out.astype(jnp.float32).astype(jnp.bfloat16), "tp", scatter_dimension=0, tiled=True
    ).astype(jnp.float32)
    own_sums = own_sums.reshape(sections, expert_groups, capacity, width)
    back_rows = exchange_both(
        own_sums.astype(jnp.bfloat16), GRP_SEC, (GRP, "sec"), (1, 0), (1, 0)
    ).astype(own_sums.dtype)
    expert_sums = back_rows.reshape(experts * capacity, width)
    expert_mix = jnp.dot(combine_rows, expert_sums, precision=lax.Precision.HIGHEST)
    return (residual + expert_mix).astype(jnp.bfloat16)


def solution(mesh):
    torus = Mesh(
        mesh.devices.reshape(mesh.shape["sec"], 8, 2, mesh.shape["tp"]),
        ("sec", "grp_0", "grp_1", "tp"),
    )
    in_specs = (
        P(SEC_GRP_TP, None),
        P(SEC_GRP, None, "tp", None),
        P(SEC_GRP, None, None),
        P(SEC_GRP),
        P(None, "tp", None, None),
        P(None, "tp", None, GRP),
        P(),
        P(),
        P(SEC_GRP_TP, None),
        P(SEC_GRP_TP),
        P(SEC_GRP, None, None, "tp"),
        P(SEC_GRP, "tp", None),
    )
    out_specs = P(SEC_GRP_TP, None)
    return jax.shard_map(
        shards, mesh=torus, in_specs=in_specs, out_specs=out_specs, check_vma=False
    )
```

profile of v0, /device:TPU:8, one launch (start us, length us, event | category | flops | bytes accessed | tf_op | source)
XLA Modules:
  0.0 292.9 jit_solution(1517495895846176154)
XLA Ops:
  6.5 0.9 iota_compare_fusion.1
  7.4 2.9 fusion.29
  10.3 0.2 fusion.52
  10.5 2.5 fusion.19
  13.1 0.6 fusion.33
  13.7 7.5 %all_gather.9 = bf16[64,2048]{1,0:T(8,128)(2,1)} all-gather(bf16[32,2048]{1,0:T(8,128)(2,1)S(1)} %bitcast.86), channel_id=1, replica_groups=mesh['sec'=2,'grp_0'=8,'grp_1'=2,'tp'=8] {'grp_1'}, dimensions={0}, use_global_device_ids=true | all-gather | bytes 393216 | tf_op jit(solution)/shard_map/all_gather | solution.py:18
  21.3 0.0 all-gather.3.cloned.1.call-update
  21.9 3.9 %copy.34 = bf16[16,1,128,448]{2,0,3,1:T(8,128)(2,1)} copy(bf16[16,1,128,448]{2,3,1,0:T(8,128)(2,1)} %param.17) | data formatting | bytes 3670016 | tf_op args[5]
  25.9 3.9 %reshape.224 = bf16[2048,448,1,1]{0,1,2,3:T(8,128)(2,1)} reshape(bf16[16,1,128,448]{2,0,3,1:T(8,128)(2,1)} %copy.34) | data formatting | bytes 3670016 | tf_op jit(solution)/shard_map/reshape;squeeze | solution.py:105
  29.7 35.4 %all-gather.3.cloned.1.call-done = bf16[512,2048]{1,0:T(8,128)(2,1)} async-done(((bf16[64,2048]{1,0:T(8,128)(2,1)}), bf16[512,2048]{1,0:T(8,128)(2,1)}) %all-gather.3.cloned.1.call-update) | async-done | bytes 2097168 | tf_op jit(solution)/shard_map/all_gather | solution.py:18
  65.2 4.1 %dot_general.32 = bf16[16,8,4,2048]{3,2,1,0:T(4,128)(2,1)} reshape(bf16[512,2048]{1,0:T(8,128)(2,1)} %all-gather.3.cloned.1.call-done) | data formatting | bytes 4194304 | tf_op jit(solution)/shard_map/dot_general | solution.py:106
  69.3 3.6 %fusion.22 = bf16[8,16,1,4,448]{4,0,3,1,2:T(8,128)(2,1)S(1)} fusion(bf16[2048,448,1,1]{0,1,2,3:T(8,128)(2,1)} %reshape.224, bf16[16,8,4,2048]{3,2,1,0:T(4,128)(2,1)} %dot_general.32), kind=kOutput, calls=%fused_computation.19 | convolution fusion | flops 939753472 | bytes 4390912 | tf_op jit(solution)/shard_map/dot_general | solution.py:106
  72.9 1.1 copy.36
  74.0 4.3 %all-to-all-start = ((bf16[8,16,1,4,448]{4,3,1,2,0:T(4,128)(2,1)}), bf16[8,16,1,4,448]{4,3,1,2,0:T(4,128)(2,1)S(1)}, u32[]{:S(2)}, u32[]{:S(2)}) async-start(bf16[8,16,1,4,448]{4,3,1,2,0:T(4,128)(2,1)} %copy.36), calls=%async_computation | async-start | bytes 1048576 | tf_op jit(solution)/shard_map/all_to_all | solution.py:30
  78.2 0.1 fusion.47
  78.3 0.1 fusion.51
  78.5 10.1 %all-to-all-done = bf16[8,16,1,4,448]{4,3,1,2,0:T(4,128)(2,1)S(1)} async-done(((bf16[8,16,1,4,448]{4,3,1,2,0:T(4,128)(2,1)}), bf16[8,16,1,4,448]{4,3,1,2,0:T(4,128)(2,1)S(1)}, u32[]{:S(2)}, u32[]{:S(2)}) %all-to-all-start) | async-done | bytes 458784 | tf_op jit(solution)/shard_map/all_to_all | solution.py:30
  88.5 0.9 reduce_sum.58
  89.4 5.9 %all-to-all-start.1 = ((bf16[16,4,448]{2,1,0:T(4,128)(2,1)}), bf16[16,4,448]{2,1,0:T(4,128)(2,1)S(1)}, u32[]{:S(2)}, u32[]{:S(2)}) async-start(bf16[16,4,448]{2,1,0:T(4,128)(2,1)} %reduce_sum.58), calls=%async_computation.1 | async-start | bytes 131072 | tf_op jit(solution)/shard_map/all_to_all | solution.py:114
  95.4 0.0 all-gather.5.cloned.1.call-start
  95.4 0.1 copy.39
  95.5 0.1 copy.40
  95.6 10.3 %all-to-all-done.1 = bf16[16,4,448]{2,1,0:T(4,128)(2,1)S(1)} async-done(((bf16[16,4,448]{2,1,0:T(4,128)(2,1)}), bf16[16,4,448]{2,1,0:T(4,128)(2,1)S(1)}, u32[]{:S(2)}, u32[]{:S(2)}) %all-to-all-start.1) | async-done | bytes 57376 | tf_op jit(solution)/shard_map/all_to_all | solution.py:114
  106.0 0.1 reshape.222
  106.1 0.2 multiply_reduce_fusion
  106.3 0.1 multiply_convert_fusion
  106.4 1.2 fusion.38
  107.7 0.2 select_reduce_fusion
  107.9 0.1 divide_multiply_fusion
  107.9 0.1 select_reduce_fusion.2
  108.0 0.1 copy.41
  108.2 0.4 fusion.1
  108.6 0.9 copy.43
  109.5 27.3 %all_to_all.24 = bf16[32,1,1,2,7168]{4,3,2,1,0:T(2,128)(2,1)S(1)} all-to-all(bf16[32,1,1,2,7168]{4,3,2,1,0:T(2,128)(2,1)S(1)} %copy.43), channel_id=1, replica_groups=mesh['sec'=2,'grp_0'=8,'grp_1'=2,'tp'=8] {'sec','grp_0','grp_1'}, dimensions={0} | all-to-all | bytes 1835008 | tf_op jit(solution)/shard_map/all_to_all | solution.py:46
  136.9 1.3 reshape_reshape.7
  138.1 0.0 all-gather.5.cloned.1.call-update
  138.1 0.2 reduce-scatter.2.cloned.1.call-start
  138.4 43.3 %all-gather.5.cloned.1.call-done = bf16[512,7168]{1,0:T(8,128)(2,1)} async-done(((bf16[64,7168]{1,0:T(8,128)(2,1)}), bf16[512,7168]{1,0:T(8,128)(2,1)}) %all-gather.5.cloned.1.call-update) | async-done | bytes 7340048 | tf_op jit(solution)/shard_map/all_gather | solution.py:154
  181.7 6.3 %fusion.3 = f32[512,256]{1,0:T(8,128)S(1)} fusion(bf16[512,7168]{1,0:T(8,128)(2,1)} %all-gather.5.cloned.1.call-done, bf16[896,8,2,128]{3,2,1,0:T(2,128)(2,1)} %bitcast.88), kind=kOutput, calls=%fused_computation.6 | convolution fusion | flops 1879048192 | bytes 11534336 | tf_op jit(solution)/shard_map/dot_general | solution.py:54
  188.0 5.1 %convolution_convert_fusion = bf16[512,7168]{1,0:T(8,128)(2,1)} fusion(bf16[1,128,7168]{2,1,0:T(8,128)(2,1)S(1)} %copy-done.1, f32[512,256]{1,0:T(8,128)S(1)} %fusion.3), kind=kOutput, calls=%fused_computation.1 | convolution fusion | flops 943587328 | bytes 9699328 | tf_op jit(solution)/shard_map/dot_general | solution.py:60
  193.1 0.0 reduce-scatter.2.cloned.1.call-update
  193.1 50.3 %reduce-scatter.2.cloned.1.call-done = bf16[64,7168]{1,0:T(8,128)(2,1)} async-done(((bf16[512,7168]{1,0:T(8,128)(2,1)}), bf16[64,7168]{1,0:T(8,128)(2,1)}) %reduce-scatter.2.cloned.1.call-update) | async-done | bytes 917520 | tf_op jit(solution)/shard_map/reduce_scatter | solution.py:156
  243.5 2.3 convert_element_type.99
  245.8 0.6 copy.44
  246.4 34.7 %all_to_all.25 = bf16[32,1,1,2,7168]{4,3,2,1,0:T(2,128)(2,1)S(1)} all-to-all(bf16[32,1,1,2,7168]{4,3,2,1,0:T(2,128)(2,1)S(1)} %bitcast.83), channel_id=1, replica_groups=mesh['sec'=2,'grp_0'=8,'grp_1'=2,'tp'=8] {'grp_0','grp_1','sec'}, dimensions={0} | all-to-all | bytes 1835008 | tf_op jit(solution)/shard_map/all_to_all | solution.py:46
  281.1 1.6 copy.67
  282.7 2.5 reshape.221
  285.2 1.2 fusion.2
  (19 shorter events, 0.2 us)
Async XLA Ops:
  6.5 6.6 %copy-start = (bf16[16,1,512,128]{3,2,1,0:T(8,128)(2,1)S(1)}, bf16[16,1,512,128]{3,2,1,0:T(8,128)(2,1)}, u32[]{:S(2)}) copy-start(bf16[16,1,512,128]{3,2,1,0:T(8,128)(2,1)} %param.16) | copy-start | bytes 6291460
  6.5 58.6 %all-gather.3.cloned.1.call-start = ((), (), s32[]{:S(2)}) async-start(), calls=%async_computation.5 | async-start | bytes 2359296 | tf_op jit(solution)/shard_map/all_gather | solution.py:18
  72.9 5.4 %copy-start.4 = (s32[4,8]{1,0:T(4,128)S(1)}, s32[4,8]{1,0:T(4,128)}, u32[]{:S(2)}) copy-start(s32[4,8]{1,0:T(4,128)} %param.20) | copy-start | bytes 388
  72.9 33.2 %copy-start.2 = (bf16[4,7168]{1,0:T(4,128)(2,1)S(1)}, bf16[4,7168]{1,0:T(4,128)(2,1)}, u32[]{:S(2)}) copy-start(bf16[4,7168]{1,0:T(4,128)(2,1)} %param.12) | copy-start | bytes 172036
  72.9 33.4 %copy-start.3 = (f32[7168]{0:T(1024)S(1)}, f32[7168]{0:T(1024)}, u32[]{:S(2)}) copy-start(f32[7168]{0:T(1024)} %param.18) | copy-start | bytes 86020
  74.0 14.6 %all-to-all-start = ((bf16[8,16,1,4,448]{4,3,1,2,0:T(4,128)(2,1)}), bf16[8,16,1,4,448]{4,3,1,2,0:T(4,128)(2,1)S(1)}, u32[]{:S(2)}, u32[]{:S(2)}) async-start(bf16[8,16,1,4,448]{4,3,1,2,0:T(4,128)(2,1)} %copy.36), calls=%async_computation | async-start | bytes 1048576 | tf_op jit(solution)/shard_map/all_to_all | solution.py:30
  89.4 16.5 %all-to-all-start.1 = ((bf16[16,4,448]{2,1,0:T(4,128)(2,1)}), bf16[16,4,448]{2,1,0:T(4,128)(2,1)S(1)}, u32[]{:S(2)}, u32[]{:S(2)}) async-start(bf16[16,4,448]{2,1,0:T(4,128)(2,1)} %reduce_sum.58), calls=%async_computation.1 | async-start | bytes 131072 | tf_op jit(solution)/shard_map/all_to_all | solution.py:114
  95.4 86.3 %all-gather.5.cloned.1.call-start = ((), (), s32[]{:S(2)}) async-start(), calls=%async_computation.6 | async-start | bytes 8257536 | tf_op jit(solution)/shard_map/all_gather | solution.py:154
  138.1 105.3 %reduce-scatter.2.cloned.1.call-start = ((), (), s32[]{:S(2)}) async-start(), calls=%async_computation.7 | async-start | bytes 8257536 | tf_op jit(solution)/shard_map/reduce_scatter | solution.py:156
  181.7 6.3 %copy-start.1 = (bf16[1,128,7168]{2,1,0:T(8,128)(2,1)S(1)}, bf16[1,128,7168]{2,1,0:T(8,128)(2,1)}, u32[]{:S(2)}) copy-start(bf16[1,128,7168]{2,1,0:T(8,128)(2,1)} %param.23) | copy-start | bytes 5505028
Sparse Core Ops, SparseCore 0:
  21.4 43.7 all-gather.2
  138.3 43.3 all-gather.4
  193.2 50.1 reduce-scatter.1
where the time goes:
time: 294 us; the launch traced here: 293 us
  waiting for transfers between devices  150 us (51%)
  blocking collectives  69.6 us (24%)
  matrix products  23.8 us (8%)
  local copies, waits for them, and re-layouts  22.7 us (8%)
  between operations  14 us (5%)
  starting transfers between devices  10.5 us (4%)
    all_to_all x2, blocking collectives, exchange_both(): tiles = lax.all_to_all(tiles, axis, split_axis=0, concat_axis=0, tiled=True)  62 us
    reduce_scatter x1, waiting for transfers between devices, shards(): lax.psum_scatter(every_out.astype(jnp.float32).astype(jnp.bfloat16), 'tp'...  50.3 us
    all_gather x1, waiting for transfers between devices, shards(): lax.all_gather(local_rows, 'tp', axis=0, tiled=True)  43.3 us
    all_gather x1, waiting for transfers between devices, gathered_by_axis(): out = lax.all_gather(out, axes[number], axis=dim, tiled=True)  35.4 us
    all_to_all x1, waiting for transfers between devices, shards(): lax.all_to_all(column_part, GRP, split_axis=0, concat_axis=2, tiled=True)[0]  10.3 us
    all_to_all x1, waiting for transfers between devices, sent_and_summed(): lax.all_to_all(tiles, axis, split_axis=0, concat_axis=0, tiled=True)  10.1 us
    all_gather x1, blocking collectives, gathered_by_axis(): out = lax.all_gather(out, axes[number], axis=dim, tiled=True)  7.51 us
    dot_general x1, matrix products, expert_slice(): jnp.dot(rows_in, expert_in[0].reshape(width, 2 * slice_width), preferred_...  6.32 us
  transfers between devices with their start and end apart: 5, of which 5 were waited for; matrix products, arithmetic and copies ran while one was open for 3% of the time, Pallas kernels for 0%

commit v1 on v0

--- a/solution.py
+++ b/solution.py
@@ -10,6 +10,12 @@
 SEC_GRP_TP = ("sec", "grp_0", "grp_1", "tp")
 score_scale = 192.0 ** (-0.5)
 route_scale = 2.5
+
+
+def stacked_exchange(x, name, split, join):
+    shards = jnp.split(x, lax.axis_size(name), axis=split)
+    received = lax.all_to_all(jnp.stack(shards), name, 0, 0)
+    return jnp.concatenate(received, axis=join)
 
 
 def gathered_by_axis(x, axes, dim):
@@ -111,7 +117,7 @@
     )
     summed = sent_and_summed(partial_value.astype(jnp.bfloat16), "tp", 1)
     column_part = summed[:, 0].astype(jnp.bfloat16)
-    attention = lax.all_to_all(column_part, GRP, split_axis=0, concat_axis=2, tiled=True)[0]
+    attention = stacked_exchange(column_part, GRP, 0, 2)[0]
     residual = hidden_in.astype(jnp.float32) + attention.astype(jnp.float32)
     normalized_input = (
         residual

time: 294 us -> 302 us (1.027)
  local copies, waits for them, and re-layouts: 22.7 us -> 32.2 us
    unnamed x11 -> x26, local copies, waits for them, and re-layouts: 3.95 us -> 12.9 us
where the time goes in v1:
time: 302 us
  waiting for transfers between devices  150 us (50%)
  blocking collectives  69.5 us (23%)
  local copies, waits for them, and re-layouts  32.2 us (11%)
  matrix products  23.8 us (8%)
  between operations  14 us (5%)
  starting transfers between devices  10.5 us (3%)
    all_to_all x2, blocking collectives, exchange_both(): tiles = lax.all_to_all(tiles, axis, split_axis=0, concat_axis=0, tiled=True)  62 us
    reduce_scatter x1, waiting for transfers between devices, shards(): lax.psum_scatter(every_out.astype(jnp.float32).astype(jnp.bfloat16), 'tp'...  50.3 us
    all_gather x1, waiting for transfers between devices, shards(): lax.all_gather(local_rows, 'tp', axis=0, tiled=True)  43.3 us
    all_gather x1, waiting for transfers between devices, gathered_by_axis(): out = lax.all_gather(out, axes[number], axis=dim, tiled=True)  35.4 us
    unnamed x26, local copies, waits for them, and re-layouts  12.9 us
    all_to_all x1, waiting for transfers between devices, stacked_exchange(): received = lax.all_to_all(jnp.stack(shards), name, 0, 0)  10.3 us
    all_to_all x1, waiting for transfers between devices, sent_and_summed(): lax.all_to_all(tiles, axis, split_axis=0, concat_axis=0, tiled=True)  10.1 us
    all_gather x1, blocking collectives, gathered_by_axis(): out = lax.all_gather(out, axes[number], axis=dim, tiled=True)  7.51 us
  transfers between devices with their start and end apart: 5, of which 5 were waited for; matrix products, arithmetic and copies ran while one was open for 3% of the time, Pallas kernels for 0%

profile of v1, /device:TPU:8, one launch (start us, length us, event | category | flops | bytes accessed | tf_op | source)
XLA Modules:
  0.0 301.7 jit_solution(16221769283066514143)
XLA Ops:
  6.5 0.9 iota_compare_fusion.1
  7.4 2.9 fusion.29
  10.3 0.2 fusion.52
  10.5 2.5 fusion.19
  13.1 0.6 fusion.33
  13.7 7.5 %all_gather.9 = bf16[64,2048]{1,0:T(8,128)(2,1)} all-gather(bf16[32,2048]{1,0:T(8,128)(2,1)S(1)} %bitcast.147), channel_id=1, replica_groups=mesh['sec'=2,'grp_0'=8,'grp_1'=2,'tp'=8] {'grp_1'}, dimensions={0}, use_global_device_ids=true | all-gather | bytes 393216 | tf_op jit(solution)/shard_map/all_gather | solution.py:24
  21.9 3.9 %copy.49 = bf16[16,1,128,448]{2,0,3,1:T(8,128)(2,1)} copy(bf16[16,1,128,448]{2,3,1,0:T(8,128)(2,1)} %param.17) | data formatting | bytes 3670016 | tf_op args[5]
  25.9 3.9 %reshape.221 = bf16[2048,448,1,1]{0,1,2,3:T(8,128)(2,1)} reshape(bf16[16,1,128,448]{2,0,3,1:T(8,128)(2,1)} %copy.49) | data formatting | bytes 3670016 | tf_op jit(solution)/shard_map/reshape;squeeze | solution.py:111
  29.7 35.4 %all-gather.3.cloned.1.call-done = bf16[512,2048]{1,0:T(8,128)(2,1)} async-done(((bf16[64,2048]{1,0:T(8,128)(2,1)}), bf16[512,2048]{1,0:T(8,128)(2,1)}) %all-gather.3.cloned.1.call-update) | async-done | bytes 2097168 | tf_op jit(solution)/shard_map/all_gather | solution.py:24
  65.2 4.1 %dot_general.32 = bf16[16,8,4,2048]{3,2,1,0:T(4,128)(2,1)} reshape(bf16[512,2048]{1,0:T(8,128)(2,1)} %all-gather.3.cloned.1.call-done) | data formatting | bytes 4194304 | tf_op jit(solution)/shard_map/dot_general | solution.py:112
  69.3 3.6 %fusion.22 = bf16[8,16,1,4,448]{4,0,3,1,2:T(8,128)(2,1)S(1)} fusion(bf16[2048,448,1,1]{0,1,2,3:T(8,128)(2,1)} %reshape.221, bf16[16,8,4,2048]{3,2,1,0:T(4,128)(2,1)} %dot_general.32), kind=kOutput, calls=%fused_computation.19 | convolution fusion | flops 939753472 | bytes 4390912 | tf_op jit(solution)/shard_map/dot_general | solution.py:112
  72.9 1.1 copy.51
  74.0 4.3 %all-to-all-start = ((bf16[8,16,1,4,448]{4,3,1,2,0:T(4,128)(2,1)}), bf16[8,16,1,4,448]{4,3,1,2,0:T(4,128)(2,1)S(1)}, u32[]{:S(2)}, u32[]{:S(2)}) async-start(bf16[8,16,1,4,448]{4,3,1,2,0:T(4,128)(2,1)} %copy.51), calls=%async_computation | async-start | bytes 1048576 | tf_op jit(solution)/shard_map/all_to_all | solution.py:36
  78.5 10.1 %all-to-all-done = bf16[8,16,1,4,448]{4,3,1,2,0:T(4,128)(2,1)S(1)} async-done(((bf16[8,16,1,4,448]{4,3,1,2,0:T(4,128)(2,1)}), bf16[8,16,1,4,448]{4,3,1,2,0:T(4,128)(2,1)S(1)}, u32[]{:S(2)}, u32[]{:S(2)}) %all-to-all-start) | async-done | bytes 458784 | tf_op jit(solution)/shard_map/all_to_all | solution.py:36
  88.5 0.3 reduce_sum.58
  88.8 0.6 constant_dynamic-update-slice_fusion.15
  89.4 0.6 constant_dynamic-update-slice_fusion.14
  90.0 0.6 constant_dynamic-update-slice_fusion.13
  90.6 0.6 constant_dynamic-update-slice_fusion.12
  91.2 0.6 constant_dynamic-update-slice_fusion.11
  91.8 0.6 constant_dynamic-update-slice_fusion.10
  92.4 0.6 constant_dynamic-update-slice_fusion.9
  93.0 0.6 constant_dynamic-update-slice_fusion.8
  93.6 0.6 constant_dynamic-update-slice_fusion.7
  94.2 0.6 constant_dynamic-update-slice_fusion.6
  94.8 0.6 constant_dynamic-update-slice_fusion.5
  95.4 0.6 constant_dynamic-update-slice_fusion.4
  95.9 0.6 constant_dynamic-update-slice_fusion.3
  96.5 0.6 constant_dynamic-update-slice_fusion.2
  97.1 0.6 constant_dynamic-update-slice_fusion.1
  97.7 0.6 constant_dynamic-update-slice_fusion
  98.3 5.9 %all-to-all-start.1 = ((bf16[16,1,4,448]{3,2,1,0:T(4,128)(2,1)}), bf16[16,1,4,448]{3,2,1,0:T(4,128)(2,1)S(1)}, u32[]{:S(2)}, u32[]{:S(2)}) async-start(bf16[16,1,4,448]{3,2,1,0:T(4,128)(2,1)} %constant_dynamic-update-slice_fusion), calls=%async_computation.1 | async-start | bytes 131072 | tf_op jit(solution)/shard_map/all_to_all | solution.py:17
  104.5 10.3 %all-to-all-done.1 = bf16[16,1,4,448]{3,2,1,0:T(4,128)(2,1)S(1)} async-done(((bf16[16,1,4,448]{3,2,1,0:T(4,128)(2,1)}), bf16[16,1,4,448]{3,2,1,0:T(4,128)(2,1)S(1)}, u32[]{:S(2)}, u32[]{:S(2)}) %all-to-all-start.1) | async-done | bytes 57376 | tf_op jit(solution)/shard_map/all_to_all | solution.py:17
  115.3 1.2 fusion.38
  117.1 0.4 fusion.1
  117.4 0.9 copy.57
  118.4 27.3 %all_to_all.20 = bf16[32,1,1,2,7168]{4,3,2,1,0:T(2,128)(2,1)S(1)} all-to-all(bf16[32,1,1,2,7168]{4,3,2,1,0:T(2,128)(2,1)S(1)} %copy.57), channel_id=1, replica_groups=mesh['sec'=2,'grp_0'=8,'grp_1'=2,'tp'=8] {'sec','grp_0','grp_1'}, dimensions={0} | all-to-all | bytes 1835008 | tf_op jit(solution)/shard_map/all_to_all | solution.py:52
  145.7 1.3 reshape_reshape.7
  147.3 43.3 %all-gather.5.cloned.1.call-done = bf16[512,7168]{1,0:T(8,128)(2,1)} async-done(((bf16[64,7168]{1,0:T(8,128)(2,1)}), bf16[512,7168]{1,0:T(8,128)(2,1)}) %all-gather.5.cloned.1.call-update) | async-done | bytes 7340048 | tf_op jit(solution)/shard_map/all_gather | solution.py:160
  190.6 6.3 %fusion.3 = f32[512,256]{1,0:T(8,128)S(1)} fusion(bf16[512,7168]{1,0:T(8,128)(2,1)} %all-gather.5.cloned.1.call-done, bf16[896,8,2,128]{3,2,1,0:T(2,128)(2,1)} %bitcast.149), kind=kOutput, calls=%fused_computation.6 | convolution fusion | flops 1879048192 | bytes 11534336 | tf_op jit(solution)/shard_map/dot_general | solution.py:60
  196.9 5.1 %convolution_convert_fusion = bf16[512,7168]{1,0:T(8,128)(2,1)} fusion(bf16[1,128,7168]{2,1,0:T(8,128)(2,1)S(1)} %copy-done.1, f32[512,256]{1,0:T(8,128)S(1)} %fusion.3), kind=kOutput, calls=%fused_computation.1 | convolution fusion | flops 943587328 | bytes 9699328 | tf_op jit(solution)/shard_map/dot_general | solution.py:66
  202.0 50.3 %reduce-scatter.2.cloned.1.call-done = bf16[64,7168]{1,0:T(8,128)(2,1)} async-done(((bf16[512,7168]{1,0:T(8,128)(2,1)}), bf16[64,7168]{1,0:T(8,128)(2,1)}) %reduce-scatter.2.cloned.1.call-update) | async-done | bytes 917520 | tf_op jit(solution)/shard_map/reduce_scatter | solution.py:162
  252.3 2.3 convert_element_type.95
  254.7 0.6 copy.58
  255.3 34.7 %all_to_all.21 = bf16[32,1,1,2,7168]{4,3,2,1,0:T(2,128)(2,1)S(1)} all-to-all(bf16[32,1,1,2,7168]{4,3,2,1,0:T(2,128)(2,1)S(1)} %bitcast.144), channel_id=1, replica_groups=mesh['sec'=2,'grp_0'=8,'grp_1'=2,'tp'=8] {'grp_0','grp_1','sec'}, dimensions={0} | all-to-all | bytes 1835008 | tf_op jit(solution)/shard_map/all_to_all | solution.py:52
  290.0 1.6 copy.80
  291.6 2.5 reshape.219
  294.0 1.2 fusion.2
  (35 shorter events, 1.7 us)
Async XLA Ops:
  6.5 6.6 %copy-start = (bf16[16,1,512,128]{3,2,1,0:T(8,128)(2,1)S(1)}, bf16[16,1,512,128]{3,2,1,0:T(8,128)(2,1)}, u32[]{:S(2)}) copy-start(bf16[16,1,512,128]{3,2,1,0:T(8,128)(2,1)} %param.16) | copy-start | bytes 6291460
  6.5 58.6 %all-gather.3.cloned.1.call-start = ((), (), s32[]{:S(2)}) async-start(), calls=%async_computation.5 | async-start | bytes 2359296 | tf_op jit(solution)/shard_map/all_gather | solution.py:24
  72.9 5.4 %copy-start.4 = (s32[4,8]{1,0:T(4,128)S(1)}, s32[4,8]{1,0:T(4,128)}, u32[]{:S(2)}) copy-start(s32[4,8]{1,0:T(4,128)} %param.20) | copy-start | bytes 388
  72.9 42.1 %copy-start.2 = (bf16[4,7168]{1,0:T(4,128)(2,1)S(1)}, bf16[4,7168]{1,0:T(4,128)(2,1)}, u32[]{:S(2)}) copy-start(bf16[4,7168]{1,0:T(4,128)(2,1)} %param.12) | copy-start | bytes 172036
  72.9 42.3 %copy-start.3 = (f32[7168]{0:T(1024)S(1)}, f32[7168]{0:T(1024)}, u32[]{:S(2)}) copy-start(f32[7168]{0:T(1024)} %param.18) | copy-start | bytes 86020
  74.0 14.6 %all-to-all-start = ((bf16[8,16,1,4,448]{4,3,1,2,0:T(4,128)(2,1)}), bf16[8,16,1,4,448]{4,3,1,2,0:T(4,128)(2,1)S(1)}, u32[]{:S(2)}, u32[]{:S(2)}) async-start(bf16[8,16,1,4,448]{4,3,1,2,0:T(4,128)(2,1)} %copy.51), calls=%async_computation | async-start | bytes 1048576 | tf_op jit(solution)/shard_map/all_to_all | solution.py:36
  98.3 16.5 %all-to-all-start.1 = ((bf16[16,1,4,448]{3,2,1,0:T(4,128)(2,1)}), bf16[16,1,4,448]{3,2,1,0:T(4,128)(2,1)S(1)}, u32[]{:S(2)}, u32[]{:S(2)}) async-start(bf16[16,1,4,448]{3,2,1,0:T(4,128)(2,1)} %constant_dynamic-update-slice_fusion), calls=%async_computation.1 | async-start | bytes 131072 | tf_op jit(solution)/shard_map/all_to_all | solution.py:17
  104.3 86.3 %all-gather.5.cloned.1.call-start = ((), (), s32[]{:S(2)}) async-start(), calls=%async_computation.6 | async-start | bytes 8257536 | tf_op jit(solution)/shard_map/all_gather | solution.py:160
  147.0 105.3 %reduce-scatter.2.cloned.1.call-start = ((), (), s32[]{:S(2)}) async-start(), calls=%async_computation.7 | async-start | bytes 8257536 | tf_op jit(solution)/shard_map/reduce_scatter | solution.py:162
  190.6 6.3 %copy-start.1 = (bf16[1,128,7168]{2,1,0:T(8,128)(2,1)S(1)}, bf16[1,128,7168]{2,1,0:T(8,128)(2,1)}, u32[]{:S(2)}) copy-start(bf16[1,128,7168]{2,1,0:T(8,128)(2,1)} %param.23) | copy-start | bytes 5505028
Sparse Core Ops, SparseCore 0:
  21.4 43.7 all-gather.2
  147.2 43.3 all-gather.4
  202.1 50.1 reduce-scatter.1
